TPU v7x, 32 devices: a whole 2x2x4 slice. The times are simulated.
32 devices in a mesh: frame: 8 (over z, x), feat: 4 (over y, core).
Axes of the slice: x: 2, y: 2, z: 4, core: 2. Of those that a mesh axis runs over, the one named last changes fastest.
Arguments:
- coords: bfloat16 [8, 64, 3, 128], P('frame', 'feat'), may hold values from -9 to 9
- walker_map: int32 [8, 64], P('frame', 'feat'), may hold values from 0 to 63, each once within a row
- pairs: int32 [2, 16384], P(None, 'feat'), may hold values from 0 to 127, as said below
Outputs:
- inst_cov: float32 [16384, 16384], P('feat', 'frame')
- lag_cov: float32 [16384, 16384], P('feat', 'frame')
Inputs may be any that keep to these rules, and one draw needn't show every extreme that they name: `pairs`: the two blocks of a feature differ.
All inputs are finite; a program needn't handle non-finite values.
Results may differ from a plain program's by a relative error of at most 0.0038.
Values may be sent and summed in bfloat16 or wider, within the bound.
No kernel may reach another device: no remote copies, remote signals or barrier semaphores. Data moves between devices by JAX's collectives and lax.ppermute only.
A program may use at most 128 MiB of HBM per device.

v0:
```python
import jax
import jax.numpy as jnp
from jax import lax
from jax.sharding import PartitionSpec as P


def demux(coords, walker_map):
    count = walker_map.shape[1]
    labels = jnp.arange(count, dtype=jnp.int32)
    match = walker_map[:, :, None] == labels[None, None, :]
    inverse = jnp.sum(jnp.where(match, labels[None, :, None], 0), axis=1)
    return jnp.take_along_axis(coords, inverse[:, :, None, None], axis=1)


def per_device(coords, walker_map, pairs):
    coords, walker_map = (
        lax.all_gather(coords, "frame", axis=0, tiled=True),
        lax.all_gather(walker_map, "frame", axis=0, tiled=True),
    )
    coords, walker_map, pairs = (
        lax.all_gather(coords, "feat", axis=1, tiled=True),
        lax.all_gather(walker_map, "feat", axis=1, tiled=True),
        lax.all_gather(pairs, "feat", axis=1, tiled=True),
    )
    frames_all, replicas = walker_map.shape
    block_count = coords.shape[3]
    total_features = pairs.shape[1]
    row_width = total_features // lax.axis_size("feat")
    col_width = total_features // lax.axis_size("frame")
    row_pairs = lax.dynamic_slice_in_dim(pairs, lax.axis_index("feat") * row_width, row_width, 1)
    col_pairs = lax.dynamic_slice_in_dim(pairs, lax.axis_index("frame") * col_width, col_width, 1)
    chosen = jnp.concatenate([row_pairs, col_pairs], axis=1)
    width = row_width + col_width
    block_ids = jnp.arange(block_count, dtype=jnp.int32)[:, None]
    pair_matrix = (
        (block_ids == chosen[0][None, :]).astype(jnp.float32)
        - (block_ids == chosen[1][None, :]).astype(jnp.float32)
    ).astype(jnp.bfloat16)
    walker_coords = demux(coords, walker_map)
    frame_blocks = walker_coords.reshape((frames_all // 8, 8 * replicas * 3, block_count))

    def measure(block):
        diff = jnp.dot(block, pair_matrix, preferred_element_type=jnp.float32).reshape(
            8 * replicas, 3, width
        )
        return jnp.sqrt(jnp.sum(diff * diff, axis=1))

    features = lax.map(measure, frame_blocks).reshape(frames_all, replicas, width)
    means = jnp.sum(features, axis=(0, 1)) / (frames_all * replicas)
    centered = (features - means).astype(jnp.bfloat16)
    left = centered[:, :, :row_width]
    right = centered[:, :, row_width:]
    contract = (((0,), (0,)), ((), ()))
    inst_cov = lax.dot_general(
        left.reshape(-1, row_width),
        right.reshape(-1, col_width),
        contract,
        preferred_element_type=jnp.float32,
    ) / (frames_all * replicas)
    lag_frames = frames_all // 3
    early = left[: frames_all - lag_frames].reshape(-1, row_width)
    late = right[lag_frames:].reshape(-1, col_width)
    lag_cov = lax.dot_general(early, late, contract, preferred_element_type=jnp.float32) / (
        (frames_all - lag_frames) * replicas
    )
    return (inst_cov, lag_cov)


def solution(mesh):
    in_specs = (P("frame", "feat", None, None), P("frame", "feat"), P(None, "feat"))
    out_specs = (P("feat", "frame"), P("feat", "frame"))
    return jax.shard_map(
        per_device, mesh=mesh, in_specs=in_specs, out_specs=out_specs, check_vma=False
    )
```

profile of v0, /device:TPU:0, one launch (start us, length us, event | category | flops | bytes accessed | tf_op | source)
XLA Modules:
  0.0 139.0 jit_solution(7853688593577064077)
XLA Ops:
  0.6 22.4 %all-gather = s32[8,1,16]{2,1,0:T(1,128)S(1)} all-gather(s32[1,1,16]{2,1,0:T(1,128)} %bitcast.28), channel_id=1, replica_groups=mesh['frame'=8,'feat'=4] {'frame'}, dimensions={0}, use_global_device_ids=true | all-gather | bytes 576 | tf_op jit(solution)/shard_map/all_gather | solution.py:18
  23.1 5.2 %all-gather.1 = s32[4,16,8]{1,2,0:T(8,128)S(1)} all-gather(s32[1,16,8]{1,2,0:T(8,128)S(1)} %bitcast.27), channel_id=1, replica_groups=mesh['frame'=8,'feat'=4] {'feat'}, dimensions={0}, use_global_device_ids=true | all-gather | bytes 2560 | tf_op jit(solution)/shard_map/all_gather | solution.py:22
  28.3 0.1 reshape.67
  28.4 0.1 select_reduce_fusion
  28.5 0.1 reduce_sum.33
  28.6 0.1 reshape.57
  28.7 30.8 %all_gather.17 = bf16[8,16,3,128]{3,1,2,0:T(8,128)(2,1)S(1)} all-gather(bf16[1,16,3,128]{3,1,2,0:T(8,128)(2,1)} %param.3), channel_id=1, replica_groups=mesh['frame'=8,'feat'=4] {'frame'}, dimensions={0}, use_global_device_ids=true | all-gather | bytes 110592 | tf_op jit(solution)/shard_map/all_gather | solution.py:17
  59.4 0.1 copy.13
  59.5 5.6 %all_gather.19 = s32[2,16384]{1,0:T(2,128)S(1)} all-gather(s32[2,4096]{1,0:T(2,128)} %param.5), channel_id=1, replica_groups=mesh['frame'=8,'feat'=4] {'feat'}, dimensions={1}, use_global_device_ids=true | all-gather | bytes 163840 | tf_op jit(solution)/shard_map/all_gather | solution.py:23
  65.2 7.3 %all_gather.18 = bf16[8,64,3,128]{3,2,1,0:T(4,128)(2,1)S(1)} all-gather(bf16[8,16,3,128]{3,2,1,0:T(4,128)(2,1)S(1)} %copy.13), channel_id=1, replica_groups=mesh['frame'=8,'feat'=4] {'feat'}, dimensions={1}, use_global_device_ids=true | all-gather | bytes 491520 | tf_op jit(solution)/shard_map/all_gather | solution.py:21
  72.4 2.4 %gather_fusion = bf16[512,3,128]{2,1,0:T(4,128)(2,1)S(1)} fusion(bf16[8,64,3,128]{3,2,1,0:T(4,128)(2,1)S(1)} %all_gather.18, s32[512]{0:T(512)S(1)} %reshape.57), kind=kCustom, calls=%fused_computation | custom fusion | bytes 790528 | tf_op jit(solution)/shard_map/jit(take_along_axis)/gather | solution.py:12
  74.9 1.8 %broadcast_select_fusion = bf16[512,3,128]{2,1,0:T(4,128)(2,1)S(1)} fusion(bf16[512,3,128]{2,1,0:T(4,128)(2,1)S(1)} %gather_fusion, pred[512]{0:T(512)(128)(4,1)S(1)} %compare_and_fusion), kind=kLoop, calls=%fused_computation.15 | loop fusion | flops 196608 | bytes 786944 | tf_op jit(solution)/shard_map/jit(take_along_axis)/select_n | solution.py:12
  76.7 11.0 %multiply_reduce_fusion = f32[512,6144]{1,0:T(8,128)} fusion(s32[6144]{0:T(1024)S(1)} %bitcast.25, s32[6144]{0:T(1024)S(1)} %bitcast.24, bf16[512,3,128]{2,1,0:T(4,128)(2,1)S(1)} %broadcast_select_fusion), kind=kOutput, calls=%fused_computation.1 | convolution fusion | flops 2436366336 | bytes 13025280 | tf_op jit(solution)/shard_map/while/body/eval_jaxpr/dot_general | solution.py:43
  87.6 12.6 %sqrt_reduce_fusion = (f32[6144]{0:T(1024)S(1)}, f32[512,6144]{1,0:T(8,128)}) fusion(f32[512,6144]{1,0:T(8,128)} %multiply_reduce_fusion), kind=kLoop, calls=%fused_computation.32 | loop fusion | flops 3139584 | bytes 25190400 | tf_op jit(solution)/shard_map/reduce_sum | solution.py:49
  100.2 6.0 %subtract_convert_fusion = bf16[8,64,6144]{2,1,0:T(8,128)(2,1)S(1)} fusion(f32[8,64,6144]{2,1,0:T(8,128)} %bitcast.23, f32[6144]{0:T(1024)S(1)} %broadcast_multiply_fusion), kind=kLoop, calls=%fused_computation.4 | loop fusion | flops 6291456 | bytes 18898944 | tf_op jit(solution)/shard_map/convert_element_type | solution.py:50
  106.3 16.5 %bitcast_multiply_fusion = f32[4096,2048]{1,0:T(8,128)} fusion(bf16[8,64,6144]{2,1,0:T(8,128)(2,1)S(1)} %subtract_convert_fusion), kind=kOutput, calls=%fused_computation.2 | convolution fusion | flops 6450839552 | bytes 38273024 | tf_op jit(solution)/shard_map/dot_general | solution.py:63
  122.7 16.3 %bitcast_multiply_fusion.1 = f32[4096,2048]{1,0:T(8,128)} fusion(bf16[8,64,6144]{2,1,0:T(8,128)(2,1)S(1)} %subtract_convert_fusion), kind=kOutput, calls=%fused_computation.3 | convolution fusion | flops 8598323200 | bytes 39845888 | tf_op jit(solution)/shard_map/dot_general | solution.py:54
  (7 shorter events, 0.1 us)
where the time goes:
time: 139 us
  blocking collectives  71.3 us (51%)
  matrix products  43.7 us (31%)
  other arithmetic  20.6 us (15%)
  local copies, waits for them, and re-layouts  2.73 us (2%)
    all_gather x1, blocking collectives, per_device(): lax.all_gather(coords, 'frame', axis=0, tiled=True)  30.8 us
    all_gather x1, blocking collectives, per_device(): lax.all_gather(walker_map, 'frame', axis=0, tiled=True)  22.4 us
    dot_general x1, matrix products, per_device(): lax.dot_general(early, late, contract, preferred_element_type=jnp.float32)  16.5 us
    dot_general x1, matrix products, per_device(): lax.dot_general(left.reshape(-1, row_width), right.reshape(-1, col_width)...  16.3 us
    reduce_sum x1, other arithmetic, per_device(): means = jnp.sum(features, axis=(0, 1)) / (frames_all * replicas)  12.6 us
    dot_general x1, matrix products, measure(): jnp.dot(block, pair_matrix, preferred_element_type=jnp.float32)  11 us
    all_gather x1, blocking collectives, per_device(): lax.all_gather(coords, 'feat', axis=1, tiled=True)  7.28 us
    convert_element_type x1, other arithmetic, per_device(): centered = (features - means).astype(jnp.bfloat16)  6.04 us

commit v1 on v0

v1 whole, which is shorter than its diff:
```python
import functools

import jax
import jax.numpy as jnp
from jax import lax
from jax.experimental import pallas as pl
from jax.experimental.pallas import tpu as pltpu
from jax.sharding import PartitionSpec as P

LANES = 128


def divisor(n, most):
    return max(d for d in range(1, min(n, most) + 1) if n % d == 0)


def swap(x, axis, bit):
    n = lax.axis_size(axis)
    return lax.ppermute(x, axis, [(i, i ^ bit) for i in range(n)])


def bits_down(n):
    return [1 << b for b in reversed(range(n.bit_length() - 1))]


def gather_all(block, pairs):
    frames, feats = lax.axis_size("frame"), lax.axis_size("feat")
    f, g = lax.axis_index("frame"), lax.axis_index("feat")
    lanes = block.shape[-1]
    held = block[None]
    for bit in bits_down(frames):
        got = swap(held, "frame", bit)
        held = jnp.stack([held, got], axis=1).reshape((-1,) + block.shape)
    share = frames // feats
    width = pairs.shape[1] // share
    piece = lax.dynamic_slice_in_dim(pairs, (f % share) * width, width, 1)
    piece = piece.astype(block.dtype).reshape(-1, lanes)
    wanted = f // share
    for bit in bits_down(feats):
        rows = held.reshape(-1, lanes)
        got = swap(jnp.concatenate([rows, piece], axis=0), "feat", bit)
        held = jnp.concatenate([held, got[: rows.shape[0]].reshape(held.shape)], axis=2)
        piece = jnp.where((wanted & bit) == (g & bit), piece, got[rows.shape[0] :])
    return held, piece


def onehot_rows(pairs_ref, out_ref):
    count, blocks = out_ref.shape
    ids = lax.broadcasted_iota(jnp.int32, (blocks, LANES), 0)
    for j in range(count // LANES):
        at = pl.ds(j * LANES, LANES)
        first = (ids == pairs_ref[0:1, at]).astype(jnp.float32)
        second = (ids == pairs_ref[1:2, at]).astype(jnp.float32)
        out_ref[at, :] = (first - second).T.astype(out_ref.dtype)


def covariances(
    lag, tile, chunk, f_ref, y_ref, rows_ref, cols_ref, inst_hbm, lag_hbm,
    x_ref, xt_ref, r_ref, l_ref, feat_ref, out_ref, sems,
):
    frames, _, replicas, blocks = y_ref.shape
    samples = frames * replicas
    row_width, col_width = rows_ref.shape[0], r_ref.shape[1]
    steps, chunks = row_width // tile, col_width // chunk
    early = (frames - lag) * replicas
    late = lag * replicas
    f = f_ref[0]

    walkers = lax.broadcasted_iota(jnp.int32, (replicas, replicas), 1)
    for t in range(frames):
        slab = y_ref.at[t ^ f]
        labels = slab[3][:, :replicas].astype(jnp.int32)
        match = (labels == walkers).astype(jnp.float32).astype(jnp.bfloat16)
        for c in range(3):
            x_ref[c, t * replicas : (t + 1) * replicas, :] = lax.dot_general(
                match, slab[c], (((0,), (0,)), ((), ())), preferred_element_type=jnp.float32
            ).astype(jnp.bfloat16)
    for c in range(3):
        xt_ref[c] = x_ref[c].astype(jnp.float32).T.astype(jnp.bfloat16)

    def distances(parts):
        total = parts[0] * parts[0] + parts[1] * parts[1] + parts[2] * parts[2]
        return jnp.sqrt(total)

    ids = lax.broadcasted_iota(jnp.int32, (blocks, LANES), 0).astype(jnp.float32)
    half = col_width // LANES
    for j in range(half):
        first = cols_ref[j : j + 1, :].astype(jnp.float32)
        second = cols_ref[half + j : half + j + 1, :].astype(jnp.float32)
        pick = (ids == first).astype(jnp.float32) - (ids == second).astype(jnp.float32)
        pick = pick.astype(jnp.bfloat16)
        values = distances(
            [jnp.dot(x_ref[c], pick, preferred_element_type=jnp.float32) for c in range(3)]
        )
        mean = jnp.sum(values, axis=0, keepdims=True) * (1.0 / samples)
        r_ref[:, j * LANES : (j + 1) * LANES] = (values - mean).astype(jnp.bfloat16)

    def left(step, slot):
        pick = rows_ref[pl.ds(pl.multiple_of(step * tile, tile), tile), :]
        values = distances(
            [jnp.dot(pick, xt_ref[c], preferred_element_type=jnp.float32) for c in range(3)]
        )
        mean = jnp.sum(values, axis=1, keepdims=True) * (1.0 / samples)
        l_ref[slot] = (values - mean).astype(jnp.bfloat16)

    def copies(step, slot, n):
        rows = pl.ds(pl.multiple_of(step * tile, tile), tile)
        at = pl.ds(n * chunk, chunk)
        return [
            pltpu.make_async_copy(
                out_ref.at[slot, o, :, at], hbm.at[rows, at], sems.at[slot, o, n]
            )
            for o, hbm in enumerate((inst_hbm, lag_hbm))
        ]

    def body(step, carry):
        slot = lax.rem(step, 2)
        left(step, 0)
        for n in range(chunks):
            at = slice(n * chunk, (n + 1) * chunk)

            @pl.when(step >= 2)
            def _():
                for copy in copies(step - 2, slot, n):
                    copy.wait()

            out_ref[slot, 0, :, at] = jnp.dot(
                l_ref[0], r_ref[:, at], preferred_element_type=jnp.float32
            ) * (1.0 / samples)
            out_ref[slot, 1, :, at] = jnp.dot(
                l_ref[0, :, :early], r_ref[late:, at], preferred_element_type=jnp.float32
            ) * (1.0 / early)
            for copy in copies(step, slot, n):
                copy.start()
        return carry

    lax.fori_loop(0, steps, body, 0)
    for step in range(max(steps - 2, 0), steps):
        for n in range(chunks):
            for copy in copies(step, step % 2, n):
                copy.wait()


def per_device(coords, walker_map, pairs):
    frames, feats = lax.axis_size("frame"), lax.axis_size("feat")
    blocks = coords.shape[3]
    row_width = pairs.shape[1]
    col_width = row_width * feats // frames
    labels = jnp.broadcast_to(walker_map[0][:, None], (walker_map.shape[1], blocks))
    block = jnp.concatenate(
        [jnp.swapaxes(coords[0], 0, 1), labels.astype(coords.dtype)[None]], axis=0
    )
    rows = pl.pallas_call(
        onehot_rows,
        out_shape=jax.ShapeDtypeStruct((row_width, blocks), jnp.bfloat16),
        cost_estimate=pl.CostEstimate(
            flops=4 * row_width * blocks, bytes_accessed=2 * row_width * blocks, transcendentals=0
        ),
    )(pairs)
    held, cols = gather_all(block, pairs)
    replicas = held.shape[2]
    samples = frames * replicas
    tile, chunk = divisor(row_width, 256), divisor(col_width, 512)
    vmem = pl.BlockSpec(memory_space=pltpu.VMEM)
    hbm = pl.BlockSpec(memory_space=pl.ANY)
    return pl.pallas_call(
        functools.partial(covariances, frames // 3, tile, chunk),
        out_shape=[jax.ShapeDtypeStruct((row_width, col_width), jnp.float32)] * 2,
        in_specs=[pl.BlockSpec(memory_space=pltpu.SMEM), vmem, vmem, vmem],
        out_specs=[hbm, hbm],
        scratch_shapes=[
            pltpu.VMEM((3, samples, blocks), jnp.bfloat16),
            pltpu.VMEM((3, blocks, samples), jnp.bfloat16),
            pltpu.VMEM((samples, col_width), jnp.bfloat16),
            pltpu.VMEM((2, tile, samples), jnp.bfloat16),
            pltpu.VMEM((8, LANES), jnp.float32),
            pltpu.VMEM((2, 2, tile, col_width), jnp.float32),
            pltpu.SemaphoreType.DMA((2, 2, col_width // chunk)),
        ],
        compiler_params=pltpu.CompilerParams(vmem_limit_bytes=48 << 20),
    )(lax.axis_index("frame").astype(jnp.int32).reshape(1), held, rows, cols)


def solution(mesh):
    in_specs = (P("frame", "feat", None, None), P("frame", "feat"), P(None, "feat"))
    out_specs = (P("feat", "frame"), P("feat", "frame"))
    return jax.shard_map(
        lambda *args: tuple(per_device(*args)),
        mesh=mesh, in_specs=in_specs, out_specs=out_specs, check_vma=False,
    )
```

time: 139 us -> 66.8 us (0.48)
  blocking collectives: 71.3 us -> 0 us
  matrix products: 43.7 us -> 0 us
  Pallas kernels: 0 us -> 43.7 us
  other arithmetic: 20.6 us -> 2.25 us
  starting transfers between devices: 0 us -> 9.96 us
  waiting for transfers between devices: 0 us -> 8.52 us
    all_gather x5 -> x0, blocking collectives: 71.3 us -> none  [the longest x1 30.8 us: per_device(): lax.all_gather(coords, 'frame', axis=0, tiled=True)]
    dot_general x3 -> x0, matrix products: 43.7 us -> none  [the longest x1 16.5 us: per_device(): lax.dot_general(early, late, contract, preferred_element_type=jnp.float32)]
    pallas_call x0 -> x2, Pallas kernels: none -> 43.7 us  [the longest x1 41.5 us: per_device(): pl.pallas_call(functools.partial(covariances, frames // 3, tile, chunk),...]
    reduce_sum x2 -> x0, other arithmetic: 12.7 us -> none  [the longest x1 12.6 us: per_device(): means = jnp.sum(features, axis=(0, 1)) / (frames_all * replicas)]
    ppermute x0 -> x5, starting transfers between devices: none -> 9.96 us  [swap(): return lax.ppermute(x, axis, [(i, i ^ bit) for i in range(n)])]
    ppermute x0 -> x5, waiting for transfers between devices: none -> 8.52 us  [swap(): return lax.ppermute(x, axis, [(i, i ^ bit) for i in range(n)])]
    convert_element_type x1 -> x2, other arithmetic: 6.04 us -> 1.38 us  [the longest x1 0.72 us: gather_all(): piece = piece.astype(block.dtype).reshape(-1, lanes)]
    gather x2 -> x0, local copies, waits for them, and re-layouts: 2.51 us -> none  [demux(): return jnp.take_along_axis(coords, inverse[:, :, None, None], axis=1)]
  transfers between devices with their start and end apart: 0 -> 5, of which waited for: 0 -> 4; matrix products, arithmetic and copies ran while one was open for 0% -> 1% of each run, Pallas kernels for 0% -> 3%
where the time goes in v1:
time: 66.8 us; the launch traced here: 66.5 us
  Pallas kernels  43.7 us (65%)
  starting transfers between devices  9.96 us (15%)
  waiting for transfers between devices  8.52 us (13%)
  other arithmetic  2.25 us (3%)
  local copies, waits for them, and re-layouts  1.35 us (2%)
  between operations  0.73 us (1%)
    pallas_call x1, Pallas kernels, per_device(): pl.pallas_call(functools.partial(covariances, frames // 3, tile, chunk),...  41.5 us
    ppermute x5, starting transfers between devices, swap(): return lax.ppermute(x, axis, [(i, i ^ bit) for i in range(n)])  9.96 us
    ppermute x5, waiting for transfers between devices, swap(): return lax.ppermute(x, axis, [(i, i ^ bit) for i in range(n)])  8.52 us
    pallas_call x1, Pallas kernels, per_device(): pl.pallas_call(onehot_rows, out_shape=jax.ShapeDtypeStruct((row_width, bl...  2.25 us
  transfers between devices with their start and end apart: 5, of which 4 were waited for; matrix products, arithmetic and copies ran while one was open for 1% of the time, Pallas kernels for 3%

profile of v1, /device:TPU:0, one launch (start us, length us, event | category | flops | bytes accessed | tf_op | source)
XLA Modules:
  0.0 66.5 jit_solution(16825810914786183538)
XLA Ops:
  0.6 0.7 convert_bitcast_fusion
  1.3 0.1 broadcast_in_dim.4
  1.4 0.7 %fusion.3 = (bf16[1,1,4,16,128]{4,3,2,1,0:T(8,128)(2,1)S(1)}, bf16[1,4,16,128]{3,2,1,0:T(8,128)(2,1)S(1)}) fusion(bf16[1,16,128]{2,1,0:T(8,128)(2,1)S(1)} %broadcast_in_dim.4, bf16[3,16,128]{2,1,0:T(8,128)(2,1)} %bitcast.38), kind=kLoop, calls=%fused_computation.12 | loop fusion | flops 8192 | bytes 49152 | tf_op jit(solution)/shard_map/stack;broadcast_in_dim | solution.py:33
  2.1 4.1 %collective-permute-start = (bf16[1,4,16,128]{3,2,1,0:T(8,128)(2,1)S(1)}, bf16[1,4,16,128]{3,2,1,0:T(8,128)(2,1)S(1)}, u32[]{:S(2)}, u32[]{:S(2)}) collective-permute-start(bf16[1,4,16,128]{3,2,1,0:T(8,128)(2,1)S(1)} %get-tuple-element.5), channel_id=1, source_target_pairs={{0,16},{4,20},{8,24},{12,28},{16,0},{20,4},{24,8},{28,12},{1,17},{... | collective-permute-start | bytes 49160 | tf_op jit(solution)/shard_map/ppermute | solution.py:19
  6.1 1.7 %collective-permute-done = bf16[1,4,16,128]{3,2,1,0:T(8,128)(2,1)S(1)} collective-permute-done((bf16[1,4,16,128]{3,2,1,0:T(8,128)(2,1)S(1)}, bf16[1,4,16,128]{3,2,1,0:T(8,128)(2,1)S(1)}, u32[]{:S(2)}, u32[]{:S(2)}) %collective-permute-start) | collective-permute-done | bytes 16416 | tf_op jit(solution)/shard_map/ppermute | solution.py:19
  7.9 1.9 %collective-permute-start.1 = (bf16[2,4,16,128]{3,2,1,0:T(8,128)(2,1)S(1)}, bf16[2,4,16,128]{3,2,1,0:T(8,128)(2,1)S(1)}, u32[]{:S(2)}, u32[]{:S(2)}) collective-permute-start(bf16[2,4,16,128]{3,2,1,0:T(8,128)(2,1)S(1)} %get-tuple-element.3), channel_id=1, source_target_pairs={{0,8},{4,12},{8,0},{12,4},{16,24},{20,28},{24,16},{28,20},{1,9},{5... | collective-permute-start | bytes 98312 | tf_op jit(solution)/shard_map/ppermute | solution.py:19
  9.8 2.0 %collective-permute-done.1 = bf16[2,4,16,128]{3,2,1,0:T(8,128)(2,1)S(1)} collective-permute-done((bf16[2,4,16,128]{3,2,1,0:T(8,128)(2,1)S(1)}, bf16[2,4,16,128]{3,2,1,0:T(8,128)(2,1)S(1)}, u32[]{:S(2)}, u32[]{:S(2)}) %collective-permute-start.1) | collective-permute-done | bytes 32800 | tf_op jit(solution)/shard_map/ppermute | solution.py:19
  11.8 1.9 %collective-permute-start.2 = (bf16[4,4,16,128]{3,2,1,0:T(8,128)(2,1)S(1)}, bf16[4,4,16,128]{3,2,1,0:T(8,128)(2,1)S(1)}, u32[]{:S(2)}, u32[]{:S(2)}) collective-permute-start(bf16[4,4,16,128]{3,2,1,0:T(8,128)(2,1)S(1)} %bitcast.33), channel_id=1, source_target_pairs={{0,4},{4,0},{8,12},{12,8},{16,20},{20,16},{24,28},{28,24},{1,5},{5... | collective-permute-start | bytes 196616 | tf_op jit(solution)/shard_map/ppermute | solution.py:19
  13.7 0.7 %dynamic-slice_convert_fusion = bf16[2,2048]{1,0:T(2,128)(2,1)S(1)} fusion(s32[2,4096]{1,0:T(2,128)} %pairs_ref.1, s32[]{:T(128)S(6)} %select_n.29), kind=kLoop, calls=%fused_computation.10 | loop fusion | flops 4096 | bytes 24580 | tf_op jit(solution)/shard_map/convert_element_type | solution.py:37
  14.5 1.6 %collective-permute-done.2 = bf16[4,4,16,128]{3,2,1,0:T(8,128)(2,1)S(1)} collective-permute-done((bf16[4,4,16,128]{3,2,1,0:T(8,128)(2,1)S(1)}, bf16[4,4,16,128]{3,2,1,0:T(8,128)(2,1)S(1)}, u32[]{:S(2)}, u32[]{:S(2)}) %collective-permute-start.2) | collective-permute-done | bytes 65568 | tf_op jit(solution)/shard_map/ppermute | solution.py:19
  16.2 2.0 %collective-permute-start.3 = (bf16[544,128]{1,0:T(8,128)(2,1)S(1)}, bf16[544,128]{1,0:T(8,128)(2,1)S(1)}, u32[]{:S(2)}, u32[]{:S(2)}) collective-permute-start(bf16[544,128]{1,0:T(8,128)(2,1)S(1)} %pad_maximum_fusion.3), channel_id=1, source_target_pairs={{0,2},{1,3},{2,0},{3,1},{4,6},{5,7},{6,4},{7,5},{8,10},{9,11},{10,... | collective-permute-start | bytes 417800 | tf_op jit(solution)/shard_map/ppermute | solution.py:19
  18.1 3.1 %collective-permute-done.3 = bf16[544,128]{1,0:T(8,128)(2,1)S(1)} collective-permute-done((bf16[544,128]{1,0:T(8,128)(2,1)S(1)}, bf16[544,128]{1,0:T(8,128)(2,1)S(1)}, u32[]{:S(2)}, u32[]{:S(2)}) %collective-permute-start.3) | collective-permute-done | bytes 139296 | tf_op jit(solution)/shard_map/ppermute | solution.py:19
  21.4 0.1 collective-permute-start.4
  21.5 2.3 %shard_map.50.rows_ref = bf16[4096,128]{1,0:T(8,128)(2,1)} custom-call(s32[2,4096]{1,0:T(2,128)} %pairs_ref.1), custom_call_target="tpu_custom_call" | custom-call | flops 2097152 | bytes 1048576 | tf_op jit(solution)/shard_map/pallas_call | solution.py:153
  23.7 0.0 collective-permute-done.4
  23.8 0.1 pad_maximum_fusion.y_ref
  23.8 0.0 copy-start
  23.8 1.2 %copy-done = bf16[4096,128]{1,0:T(8,128)(2,1)S(1)} copy-done((bf16[4096,128]{1,0:T(8,128)(2,1)S(1)}, bf16[4096,128]{1,0:T(8,128)(2,1)}, u32[]{:S(2)}) %copy-start) | copy-done | bytes 1048600
  25.1 41.5 %shard_map.51 = (f32[4096,2048]{1,0:T(8,128)}, f32[4096,2048]{1,0:T(8,128)}) custom-call(s32[1]{0:T(128)} %bitcast.f_ref, bf16[8,4,64,128]{3,2,1,0:T(8,128)(2,1)S(1)} %pad_maximum_fusion.y_ref, bf16[4096,128]{1,0:T(8,128)(2,1)S(1)} %copy-done, bf16[32,128]{1,0:T(8,128)(2,1)S(1)} %slice_select_fusion.cols_ref), custom_call_target="tpu_custom_call" | custom-call | tf_op jit(solution)/shard_map/pallas_call | solution.py:166
  (12 shorter events, 0.2 us)
Async XLA Ops:
  2.1 5.8 %collective-permute-start = (bf16[1,4,16,128]{3,2,1,0:T(8,128)(2,1)S(1)}, bf16[1,4,16,128]{3,2,1,0:T(8,128)(2,1)S(1)}, u32[]{:S(2)}, u32[]{:S(2)}) collective-permute-start(bf16[1,4,16,128]{3,2,1,0:T(8,128)(2,1)S(1)} %get-tuple-element.5), channel_id=1, source_target_pairs={{0,16},{4,20},{8,24},{12,28},{16,0},{20,4},{24,8},{28,12},{1,17},{... | collective-permute-start | bytes 49160 | tf_op jit(solution)/shard_map/ppermute | solution.py:19
  7.9 3.9 %collective-permute-start.1 = (bf16[2,4,16,128]{3,2,1,0:T(8,128)(2,1)S(1)}, bf16[2,4,16,128]{3,2,1,0:T(8,128)(2,1)S(1)}, u32[]{:S(2)}, u32[]{:S(2)}) collective-permute-start(bf16[2,4,16,128]{3,2,1,0:T(8,128)(2,1)S(1)} %get-tuple-element.3), channel_id=1, source_target_pairs={{0,8},{4,12},{8,0},{12,4},{16,24},{20,28},{24,16},{28,20},{1,9},{5... | collective-permute-start | bytes 98312 | tf_op jit(solution)/shard_map/ppermute | solution.py:19
  11.8 4.3 %collective-permute-start.2 = (bf16[4,4,16,128]{3,2,1,0:T(8,128)(2,1)S(1)}, bf16[4,4,16,128]{3,2,1,0:T(8,128)(2,1)S(1)}, u32[]{:S(2)}, u32[]{:S(2)}) collective-permute-start(bf16[4,4,16,128]{3,2,1,0:T(8,128)(2,1)S(1)} %bitcast.33), channel_id=1, source_target_pairs={{0,4},{4,0},{8,12},{12,8},{16,20},{20,16},{24,28},{28,24},{1,5},{5... | collective-permute-start | bytes 196616 | tf_op jit(solution)/shard_map/ppermute | solution.py:19
  16.2 5.1 %collective-permute-start.3 = (bf16[544,128]{1,0:T(8,128)(2,1)S(1)}, bf16[544,128]{1,0:T(8,128)(2,1)S(1)}, u32[]{:S(2)}, u32[]{:S(2)}) collective-permute-start(bf16[544,128]{1,0:T(8,128)(2,1)S(1)} %pad_maximum_fusion.3), channel_id=1, source_target_pairs={{0,2},{1,3},{2,0},{3,1},{4,6},{5,7},{6,4},{7,5},{8,10},{9,11},{10,... | collective-permute-start | bytes 417800 | tf_op jit(solution)/shard_map/ppermute | solution.py:19
  21.4 2.3 %collective-permute-start.4 = (bf16[1056,128]{1,0:T(8,128)(2,1)S(1)}, bf16[1056,128]{1,0:T(8,128)(2,1)S(1)}, u32[]{:S(2)}, u32[]{:S(2)}) collective-permute-start(bf16[1056,128]{1,0:T(8,128)(2,1)S(1)} %pad_maximum_fusion.1), channel_id=1, source_target_pairs={{0,1},{1,0},{2,3},{3,2},{4,5},{5,4},{6,7},{7,6},{8,9},{9,8},{10,11... | collective-permute-start | bytes 811016 | tf_op jit(solution)/shard_map/ppermute | solution.py:19
  23.8 1.2 %copy-start = (bf16[4096,128]{1,0:T(8,128)(2,1)S(1)}, bf16[4096,128]{1,0:T(8,128)(2,1)}, u32[]{:S(2)}) copy-start(bf16[4096,128]{1,0:T(8,128)(2,1)} %shard_map.50.rows_ref) | copy-start | bytes 3145732

commit v2 on v1

v2 whole, which is shorter than its diff:
```python
import functools

import jax
import jax.numpy as jnp
from jax import lax
from jax.experimental import pallas as pl
from jax.experimental.pallas import tpu as pltpu
from jax.sharding import PartitionSpec as P

LANES = 128
TINY = 1.1754944e-38


def divisor(n, most):
    return max(d for d in range(1, min(n, most) + 1) if n % d == 0)


def swap(x, axis, bit):
    n = lax.axis_size(axis)
    return lax.ppermute(x, axis, [(i, i ^ bit) for i in range(n)])


def bits_down(n):
    return [1 << b for b in reversed(range(n.bit_length() - 1))]


def gather_all(block, pairs):
    frames, feats = lax.axis_size("frame"), lax.axis_size("feat")
    f, g = lax.axis_index("frame"), lax.axis_index("feat")
    lanes = block.shape[-1]
    held = block[None]
    for bit in bits_down(frames):
        got = swap(held, "frame", bit)
        held = jnp.stack([held, got], axis=1).reshape((-1,) + block.shape)
    share = frames // feats
    width = pairs.shape[1] // share
    piece = lax.dynamic_slice_in_dim(pairs, (f % share) * width, width, 1)
    piece = piece.astype(block.dtype).reshape(-1, lanes)
    wanted = f // share
    for bit in bits_down(feats):
        rows = held.reshape(-1, lanes)
        got = swap(jnp.concatenate([rows, piece], axis=0), "feat", bit)
        held = jnp.concatenate([held, got[: rows.shape[0]].reshape(held.shape)], axis=2)
        piece = jnp.where((wanted & bit) == (g & bit), piece, got[rows.shape[0] :])
    return held, piece


def covariances(
    lag, tile, chunk, f_ref, y_ref, pairs_ref, cols_ref, inst_hbm, lag_hbm,
    x_ref, xt_ref, r_ref, la_ref, lb_ref, out_ref, sems,
):
    frames, _, replicas, blocks = y_ref.shape
    samples = frames * replicas
    row_width, col_width = pairs_ref.shape[1], r_ref.shape[1]
    steps, chunks = row_width // tile, col_width // chunk
    early = (frames - lag) * replicas
    late = lag * replicas
    f = f_ref[0]
    sides = (la_ref, lb_ref)

    walkers = lax.broadcasted_iota(jnp.int32, (replicas, replicas), 1).astype(jnp.float32)
    for t in range(frames):
        slab = y_ref.at[t ^ f]
        labels = slab[3][:, :replicas].astype(jnp.float32)
        match = jnp.where(labels == walkers, 1.0, 0.0).astype(jnp.bfloat16)
        for c in range(3):
            part = lax.dot_general(
                match, slab[c], (((0,), (0,)), ((), ())), preferred_element_type=jnp.float32
            )
            at = (t * 3 + c) * replicas
            x_ref[at : at + replicas, :] = part.astype(jnp.bfloat16)
            xt_ref[c, t] = part.T.astype(jnp.bfloat16)

    def root(x):
        return x * lax.rsqrt(jnp.maximum(x, TINY))

    ids = lax.broadcasted_iota(jnp.int32, (blocks, LANES), 0)
    idsf = ids.astype(jnp.float32)
    half = col_width // LANES

    def pick_cols(j):
        first = cols_ref[j : j + 1, :].astype(jnp.float32)
        second = cols_ref[half + j : half + j + 1, :].astype(jnp.float32)
        return (jnp.where(idsf == first, 1.0, 0.0) - jnp.where(idsf == second, 1.0, 0.0))

    def right(n):
        wide = min(256, chunk)
        for k in range(n * chunk, (n + 1) * chunk, wide):
            pick = jnp.concatenate(
                [pick_cols(k // LANES + i) for i in range(wide // LANES)], axis=1
            ).astype(jnp.bfloat16)
            parts = jnp.dot(x_ref[...], pick, preferred_element_type=jnp.float32)
            parts = parts.reshape(frames, 3, replicas, wide)
            values = root(jnp.sum(parts * parts, axis=1)).reshape(samples, wide)
            mean = jnp.sum(values, axis=0, keepdims=True) * (1.0 / samples)
            r_ref[:, k : k + wide] = (values - mean).astype(jnp.bfloat16)

    def left(step, l_ref, part, parts):
        rows = tile // parts
        picks = []
        for j in range(rows // LANES):
            at = pl.ds(pl.multiple_of(step * tile + part * rows + j * LANES, LANES), LANES)
            first = jnp.where(ids == pairs_ref[0:1, at], 1.0, 0.0)
            second = jnp.where(ids == pairs_ref[1:2, at], 1.0, 0.0)
            picks.append((first - second).T.astype(jnp.bfloat16))
        pick = jnp.concatenate(picks, axis=0)
        total = None
        for c in range(3):
            xt = jnp.concatenate([xt_ref[c, t] for t in range(frames)], axis=1)
            d = jnp.dot(pick, xt, preferred_element_type=jnp.float32)
            total = d * d if total is None else total + d * d
        values = root(total)
        mean = jnp.sum(values, axis=1, keepdims=True) * (1.0 / samples)
        l_ref[part * rows : (part + 1) * rows, :] = (values - mean).astype(jnp.bfloat16)

    def copies(step, slot, n):
        rows = pl.ds(pl.multiple_of(step * tile, tile), tile)
        at = pl.ds(n * chunk, chunk)
        return [
            pltpu.make_async_copy(
                out_ref.at[slot, o, :, at], hbm.at[rows, at], sems.at[slot, o, n]
            )
            for o, hbm in enumerate((inst_hbm, lag_hbm))
        ]

    def products(l_ref, slot, n):
        at = slice(n * chunk, (n + 1) * chunk)
        out_ref[slot, 0, :, at] = jnp.dot(
            l_ref[...], r_ref[:, at], preferred_element_type=jnp.float32
        ) * (1.0 / samples)
        out_ref[slot, 1, :, at] = jnp.dot(
            l_ref[:, :early], r_ref[late:, at], preferred_element_type=jnp.float32
        ) * (1.0 / early)

    def round_of(step, slot, first=False, wait=True, last=False):
        if wait:
            for n in range(chunks):
                for copy in copies(step - 2, slot, n):
                    copy.wait()
        for n in range(chunks):
            products(sides[slot], slot, n)
            if first and n + 1 < chunks:
                right(n + 1)
            if not last:
                left(step + 1, sides[1 - slot], n, chunks)
            for copy in copies(step, slot, n):
                copy.start()

    left(0, la_ref, 0, 1)
    right(0)
    if steps % 2:
        raise ValueError("odd steps")
    round_of(0, 0, first=True, wait=False)
    round_of(1, 1, wait=False, last=steps == 2)
    if steps > 2:
        def body(i, carry):
            round_of(2 * i, 0)
            round_of(2 * i + 1, 1)
            return carry

        lax.fori_loop(1, steps // 2 - 1, body, 0)
        round_of(steps - 2, 0)
        round_of(steps - 1, 1, last=True)
    for step in (steps - 2, steps - 1):
        for n in range(chunks):
            for copy in copies(step, step % 2, n):
                copy.wait()


def per_device(coords, walker_map, pairs):
    frames, feats = lax.axis_size("frame"), lax.axis_size("feat")
    blocks = coords.shape[3]
    row_width = pairs.shape[1]
    col_width = row_width * feats // frames
    labels = jnp.broadcast_to(walker_map[0][:, None], (walker_map.shape[1], blocks))
    block = jnp.concatenate(
        [jnp.swapaxes(coords[0], 0, 1), labels.astype(coords.dtype)[None]], axis=0
    )
    held, cols = gather_all(block, pairs)
    replicas = held.shape[2]
    samples = frames * replicas
    tile, chunk = divisor(row_width // 2, 512), divisor(col_width, 512)
    vmem = pl.BlockSpec(memory_space=pltpu.VMEM)
    hbm = pl.BlockSpec(memory_space=pl.ANY)
    return pl.pallas_call(
        functools.partial(covariances, frames // 3, tile, chunk),
        out_shape=[jax.ShapeDtypeStruct((row_width, col_width), jnp.float32)] * 2,
        in_specs=[pl.BlockSpec(memory_space=pltpu.SMEM), vmem, vmem, vmem],
        out_specs=[hbm, hbm],
        scratch_shapes=[
            pltpu.VMEM((samples * 3, blocks), jnp.bfloat16),
            pltpu.VMEM((3, frames, blocks, replicas), jnp.bfloat16),
            pltpu.VMEM((samples, col_width), jnp.bfloat16),
            pltpu.VMEM((tile, samples), jnp.bfloat16),
            pltpu.VMEM((tile, samples), jnp.bfloat16),
            pltpu.VMEM((2, 2, tile, col_width), jnp.float32),
            pltpu.SemaphoreType.DMA((2, 2, col_width // chunk)),
        ],
        compiler_params=pltpu.CompilerParams(vmem_limit_bytes=52 << 20),
    )(lax.axis_index("frame").astype(jnp.int32).reshape(1), held, pairs, cols)


def solution(mesh):
    in_specs = (P("frame", "feat", None, None), P("frame", "feat"), P(None, "feat"))
    out_specs = (P("feat", "frame"), P("feat", "frame"))
    return jax.shard_map(
        lambda *args: tuple(per_device(*args)),
        mesh=mesh, in_specs=in_specs, out_specs=out_specs, check_vma=False,
    )
```

time: 66.8 us -> 52.3 us (0.78)
  Pallas kernels: 43.7 us -> 28 us
  waiting for transfers between devices: 8.52 us -> 10 us
    pallas_call x1, Pallas kernels: 41.5 us -> 28 us  [per_device(): pl.pallas_call(functools.partial(covariances, frames // 3, tile, chunk),...]
    pallas_call x1 -> x0, Pallas kernels: 2.25 us -> none  [per_device(): pl.pallas_call(onehot_rows, out_shape=jax.ShapeDtypeStruct((row_width, bl...]
    ppermute x5, waiting for transfers between devices: 8.52 us -> 10 us  [swap(): return lax.ppermute(x, axis, [(i, i ^ bit) for i in range(n)])]
  transfers between devices with their start and end apart: 5 -> 5, of which waited for: 4 -> 5; matrix products, arithmetic and copies ran while one was open for 1% -> 1% of each run, Pallas kernels for 3% -> 0%
where the time goes in v2:
time: 52.3 us; the launch traced here: 52 us
  Pallas kernels  28 us (54%)
  waiting for transfers between devices  10 us (19%)
  starting transfers between devices  9.96 us (19%)
  other arithmetic  2.25 us (4%)
  between operations  0.89 us (2%)
  local copies, waits for them, and re-layouts  0.88 us (2%)
    pallas_call x1, Pallas kernels, per_device(): pl.pallas_call(functools.partial(covariances, frames // 3, tile, chunk),...  28 us
    ppermute x5, waiting for transfers between devices, swap(): return lax.ppermute(x, axis, [(i, i ^ bit) for i in range(n)])  10 us
    ppermute x5, starting transfers between devices, swap(): return lax.ppermute(x, axis, [(i, i ^ bit) for i in range(n)])  9.96 us
  transfers between devices with their start and end apart: 5, of which 5 were waited for; matrix products, arithmetic and copies ran while one was open for 1% of the time, Pallas kernels for 0%

profile of v2, /device:TPU:0, one launch (start us, length us, event | category | flops | bytes accessed | tf_op | source)
XLA Modules:
  0.0 52.0 jit_solution(2263206784249916881)
XLA Ops:
  0.6 0.7 %convert_bitcast_fusion = bf16[16]{0:T(256)(128)(2,1)S(1)} fusion(s32[1,16]{1,0:T(1,128)} %param.4), kind=kLoop, calls=%fused_computation.15 | loop fusion | flops 16 | bytes 96 | tf_op jit(solution)/shard_map/convert_element_type | solution.py:177
  1.3 0.1 broadcast_in_dim.4
  1.4 0.7 %fusion.3 = (bf16[1,1,4,16,128]{4,3,2,1,0:T(8,128)(2,1)S(1)}, bf16[1,4,16,128]{3,2,1,0:T(8,128)(2,1)S(1)}) fusion(bf16[1,16,128]{2,1,0:T(8,128)(2,1)S(1)} %broadcast_in_dim.4, bf16[3,16,128]{2,1,0:T(8,128)(2,1)} %bitcast.38), kind=kLoop, calls=%fused_computation.12 | loop fusion | flops 8192 | bytes 49152 | tf_op jit(solution)/shard_map/stack;broadcast_in_dim | solution.py:34
  2.1 4.1 %collective-permute-start = (bf16[1,4,16,128]{3,2,1,0:T(8,128)(2,1)S(1)}, bf16[1,4,16,128]{3,2,1,0:T(8,128)(2,1)S(1)}, u32[]{:S(2)}, u32[]{:S(2)}) collective-permute-start(bf16[1,4,16,128]{3,2,1,0:T(8,128)(2,1)S(1)} %get-tuple-element.5), channel_id=1, source_target_pairs={{0,16},{4,20},{8,24},{12,28},{16,0},{20,4},{24,8},{28,12},{1,17},{... | collective-permute-start | bytes 49160 | tf_op jit(solution)/shard_map/ppermute | solution.py:20
  6.1 1.7 %collective-permute-done = bf16[1,4,16,128]{3,2,1,0:T(8,128)(2,1)S(1)} collective-permute-done((bf16[1,4,16,128]{3,2,1,0:T(8,128)(2,1)S(1)}, bf16[1,4,16,128]{3,2,1,0:T(8,128)(2,1)S(1)}, u32[]{:S(2)}, u32[]{:S(2)}) %collective-permute-start) | collective-permute-done | bytes 16416 | tf_op jit(solution)/shard_map/ppermute | solution.py:20
  7.9 1.9 %collective-permute-start.1 = (bf16[2,4,16,128]{3,2,1,0:T(8,128)(2,1)S(1)}, bf16[2,4,16,128]{3,2,1,0:T(8,128)(2,1)S(1)}, u32[]{:S(2)}, u32[]{:S(2)}) collective-permute-start(bf16[2,4,16,128]{3,2,1,0:T(8,128)(2,1)S(1)} %get-tuple-element.3), channel_id=1, source_target_pairs={{0,8},{4,12},{8,0},{12,4},{16,24},{20,28},{24,16},{28,20},{1,9},{5... | collective-permute-start | bytes 98312 | tf_op jit(solution)/shard_map/ppermute | solution.py:20
  9.8 2.0 %collective-permute-done.1 = bf16[2,4,16,128]{3,2,1,0:T(8,128)(2,1)S(1)} collective-permute-done((bf16[2,4,16,128]{3,2,1,0:T(8,128)(2,1)S(1)}, bf16[2,4,16,128]{3,2,1,0:T(8,128)(2,1)S(1)}, u32[]{:S(2)}, u32[]{:S(2)}) %collective-permute-start.1) | collective-permute-done | bytes 32800 | tf_op jit(solution)/shard_map/ppermute | solution.py:20
  11.8 1.9 %collective-permute-start.2 = (bf16[4,4,16,128]{3,2,1,0:T(8,128)(2,1)S(1)}, bf16[4,4,16,128]{3,2,1,0:T(8,128)(2,1)S(1)}, u32[]{:S(2)}, u32[]{:S(2)}) collective-permute-start(bf16[4,4,16,128]{3,2,1,0:T(8,128)(2,1)S(1)} %bitcast.33), channel_id=1, source_target_pairs={{0,4},{4,0},{8,12},{12,8},{16,20},{20,16},{24,28},{28,24},{1,5},{5... | collective-permute-start | bytes 196616 | tf_op jit(solution)/shard_map/ppermute | solution.py:20
  13.7 0.7 %dynamic-slice_convert_fusion = bf16[2,2048]{1,0:T(2,128)(2,1)S(1)} fusion(s32[2,4096]{1,0:T(2,128)} %pairs_ref.1, s32[]{:T(128)S(6)} %select_n.29), kind=kLoop, calls=%fused_computation.10 | loop fusion | flops 4096 | bytes 24580 | tf_op jit(solution)/shard_map/convert_element_type | solution.py:38
  14.5 1.6 %collective-permute-done.2 = bf16[4,4,16,128]{3,2,1,0:T(8,128)(2,1)S(1)} collective-permute-done((bf16[4,4,16,128]{3,2,1,0:T(8,128)(2,1)S(1)}, bf16[4,4,16,128]{3,2,1,0:T(8,128)(2,1)S(1)}, u32[]{:S(2)}, u32[]{:S(2)}) %collective-permute-start.2) | collective-permute-done | bytes 65568 | tf_op jit(solution)/shard_map/ppermute | solution.py:20
  16.2 2.0 %collective-permute-start.3 = (bf16[544,128]{1,0:T(8,128)(2,1)S(1)}, bf16[544,128]{1,0:T(8,128)(2,1)S(1)}, u32[]{:S(2)}, u32[]{:S(2)}) collective-permute-start(bf16[544,128]{1,0:T(8,128)(2,1)S(1)} %pad_maximum_fusion.3), channel_id=1, source_target_pairs={{0,2},{1,3},{2,0},{3,1},{4,6},{5,7},{6,4},{7,5},{8,10},{9,11},{10,... | collective-permute-start | bytes 417800 | tf_op jit(solution)/shard_map/ppermute | solution.py:20
  18.1 3.1 %collective-permute-done.3 = bf16[544,128]{1,0:T(8,128)(2,1)S(1)} collective-permute-done((bf16[544,128]{1,0:T(8,128)(2,1)S(1)}, bf16[544,128]{1,0:T(8,128)(2,1)S(1)}, u32[]{:S(2)}, u32[]{:S(2)}) %collective-permute-start.3) | collective-permute-done | bytes 139296 | tf_op jit(solution)/shard_map/ppermute | solution.py:20
  21.4 0.1 collective-permute-start.4
  21.5 1.5 %collective-permute-done.4 = bf16[1056,128]{1,0:T(8,128)(2,1)S(1)} collective-permute-done((bf16[1056,128]{1,0:T(8,128)(2,1)S(1)}, bf16[1056,128]{1,0:T(8,128)(2,1)S(1)}, u32[]{:S(2)}, u32[]{:S(2)}) %collective-permute-start.4) | collective-permute-done | bytes 270368 | tf_op jit(solution)/shard_map/ppermute | solution.py:20
  23.0 0.1 pad_maximum_fusion.y_ref
  23.1 0.0 copy-start
  23.1 0.7 %copy-done = s32[2,4096]{1,0:T(2,128)S(1)} copy-done((s32[2,4096]{1,0:T(2,128)S(1)}, s32[2,4096]{1,0:T(2,128)}, u32[]{:S(2)}) %copy-start) | copy-done | bytes 32792
  23.9 28.0 %shard_map.50 = (f32[4096,2048]{1,0:T(8,128)}, f32[4096,2048]{1,0:T(8,128)}) custom-call(s32[1]{0:T(128)} %bitcast.f_ref, bf16[8,4,64,128]{3,2,1,0:T(8,128)(2,1)S(1)} %pad_maximum_fusion.y_ref, s32[2,4096]{1,0:T(2,128)S(1)} %copy-done, bf16[32,128]{1,0:T(8,128)(2,1)S(1)} %slice_select_fusion.cols_ref), custom_call_target="tpu_custom_call" | custom-call | tf_op jit(solution)/shard_map/pallas_call | solution.py:185
  (12 shorter events, 0.2 us)
Async XLA Ops:
  2.1 5.8 %collective-permute-start = (bf16[1,4,16,128]{3,2,1,0:T(8,128)(2,1)S(1)}, bf16[1,4,16,128]{3,2,1,0:T(8,128)(2,1)S(1)}, u32[]{:S(2)}, u32[]{:S(2)}) collective-permute-start(bf16[1,4,16,128]{3,2,1,0:T(8,128)(2,1)S(1)} %get-tuple-element.5), channel_id=1, source_target_pairs={{0,16},{4,20},{8,24},{12,28},{16,0},{20,4},{24,8},{28,12},{1,17},{... | collective-permute-start | bytes 49160 | tf_op jit(solution)/shard_map/ppermute | solution.py:20
  7.9 3.9 %collective-permute-start.1 = (bf16[2,4,16,128]{3,2,1,0:T(8,128)(2,1)S(1)}, bf16[2,4,16,128]{3,2,1,0:T(8,128)(2,1)S(1)}, u32[]{:S(2)}, u32[]{:S(2)}) collective-permute-start(bf16[2,4,16,128]{3,2,1,0:T(8,128)(2,1)S(1)} %get-tuple-element.3), channel_id=1, source_target_pairs={{0,8},{4,12},{8,0},{12,4},{16,24},{20,28},{24,16},{28,20},{1,9},{5... | collective-permute-start | bytes 98312 | tf_op jit(solution)/shard_map/ppermute | solution.py:20
  11.8 4.3 %collective-permute-start.2 = (bf16[4,4,16,128]{3,2,1,0:T(8,128)(2,1)S(1)}, bf16[4,4,16,128]{3,2,1,0:T(8,128)(2,1)S(1)}, u32[]{:S(2)}, u32[]{:S(2)}) collective-permute-start(bf16[4,4,16,128]{3,2,1,0:T(8,128)(2,1)S(1)} %bitcast.33), channel_id=1, source_target_pairs={{0,4},{4,0},{8,12},{12,8},{16,20},{20,16},{24,28},{28,24},{1,5},{5... | collective-permute-start | bytes 196616 | tf_op jit(solution)/shard_map/ppermute | solution.py:20
  16.2 5.1 %collective-permute-start.3 = (bf16[544,128]{1,0:T(8,128)(2,1)S(1)}, bf16[544,128]{1,0:T(8,128)(2,1)S(1)}, u32[]{:S(2)}, u32[]{:S(2)}) collective-permute-start(bf16[544,128]{1,0:T(8,128)(2,1)S(1)} %pad_maximum_fusion.3), channel_id=1, source_target_pairs={{0,2},{1,3},{2,0},{3,1},{4,6},{5,7},{6,4},{7,5},{8,10},{9,11},{10,... | collective-permute-start | bytes 417800 | tf_op jit(solution)/shard_map/ppermute | solution.py:20
  21.4 1.6 %collective-permute-start.4 = (bf16[1056,128]{1,0:T(8,128)(2,1)S(1)}, bf16[1056,128]{1,0:T(8,128)(2,1)S(1)}, u32[]{:S(2)}, u32[]{:S(2)}) collective-permute-start(bf16[1056,128]{1,0:T(8,128)(2,1)S(1)} %pad_maximum_fusion.1), channel_id=1, source_target_pairs={{0,1},{1,0},{2,3},{3,2},{4,5},{5,4},{6,7},{7,6},{8,9},{9,8},{10,11... | collective-permute-start | bytes 811016 | tf_op jit(solution)/shard_map/ppermute | solution.py:20
  23.1 0.8 %copy-start = (s32[2,4096]{1,0:T(2,128)S(1)}, s32[2,4096]{1,0:T(2,128)}, u32[]{:S(2)}) copy-start(s32[2,4096]{1,0:T(2,128)} %pairs_ref.1) | copy-start | bytes 98308

commit v3 on v2

--- a/solution.py
+++ b/solution.py
@@ -29,24 +29,43 @@
     f, g = lax.axis_index("frame"), lax.axis_index("feat")
     lanes = block.shape[-1]
     held = block[None]
-    for bit in bits_down(frames):
+    for bit in bits_down(frames)[:-1]:
         got = swap(held, "frame", bit)
         held = jnp.stack([held, got], axis=1).reshape((-1,) + block.shape)
     share = frames // feats
     width = pairs.shape[1] // share
     piece = lax.dynamic_slice_in_dim(pairs, (f % share) * width, width, 1)
-    piece = piece.astype(block.dtype).reshape(-1, lanes)
+    piece = piece.reshape(-1, lanes)
     wanted = f // share
-    for bit in bits_down(feats):
+
+    def feat_hop(held, piece, bit):
         rows = held.reshape(-1, lanes)
         got = swap(jnp.concatenate([rows, piece], axis=0), "feat", bit)
-        held = jnp.concatenate([held, got[: rows.shape[0]].reshape(held.shape)], axis=2)
         piece = jnp.where((wanted & bit) == (g & bit), piece, got[rows.shape[0] :])
-    return held, piece
+        return got[: rows.shape[0]].reshape(held.shape), piece
+
+    def corner(x):
+        both = [
+            (i * feats + j, (i ^ 1) * feats + (j ^ 2)) for i in range(frames) for j in range(feats)
+        ]
+        return lax.ppermute(x, ("frame", "feat"), both)
+
+    for bit in bits_down(feats)[:-2]:
+        got, piece = feat_hop(held, piece, bit)
+        held = jnp.concatenate([held, got], axis=2)
+    far = corner(held)
+    near, piece = feat_hop(held, piece, 2)
+    side = swap(held, "frame", 1)
+    held = jnp.stack(
+        [jnp.concatenate([held, near], axis=2), jnp.concatenate([side, far], axis=2)], axis=1
+    )
+    held = held.reshape((frames,) + held.shape[2:])
+    got, piece = feat_hop(held, piece, 1)
+    return jnp.concatenate([held, got], axis=2), piece
 
 
 def covariances(
-    lag, tile, chunk, f_ref, y_ref, pairs_ref, cols_ref, inst_hbm, lag_hbm,
+    lag, count, tile, chunk, f_ref, y_ref, pairs_ref, cols_ref, inst_hbm, lag_hbm,
     x_ref, xt_ref, r_ref, la_ref, lb_ref, out_ref, sems,
 ):
     frames, _, replicas, blocks = y_ref.shape
@@ -58,15 +77,15 @@
     f = f_ref[0]
     sides = (la_ref, lb_ref)
 
-    walkers = lax.broadcasted_iota(jnp.int32, (replicas, replicas), 1).astype(jnp.float32)
+    walkers = lax.broadcasted_iota(jnp.int32, (replicas, blocks), 0).astype(jnp.float32)
     for t in range(frames):
         slab = y_ref.at[t ^ f]
-        labels = slab[3][:, :replicas].astype(jnp.float32)
-        match = jnp.where(labels == walkers, 1.0, 0.0).astype(jnp.bfloat16)
+        labels = slab[3, 0:1, :].astype(jnp.float32)
+        for b in range(count, replicas, count):
+            labels += pltpu.roll(slab[3, b : b + 1, :].astype(jnp.float32), b, 1)
+        match = jnp.where(labels == walkers, 1.0, 0.0)[:, :replicas].astype(jnp.bfloat16)
         for c in range(3):
-            part = lax.dot_general(
-                match, slab[c], (((0,), (0,)), ((), ())), preferred_element_type=jnp.float32
-            )
+            part = jnp.dot(match, slab[c], preferred_element_type=jnp.float32)
             at = (t * 3 + c) * replicas
             x_ref[at : at + replicas, :] = part.astype(jnp.bfloat16)
             xt_ref[c, t] = part.T.astype(jnp.bfloat16)
@@ -74,8 +93,7 @@
     def root(x):
         return x * lax.rsqrt(jnp.maximum(x, TINY))
 
-    ids = lax.broadcasted_iota(jnp.int32, (blocks, LANES), 0)
-    idsf = ids.astype(jnp.float32)
+    idsf = lax.broadcasted_iota(jnp.int32, (blocks, LANES), 0).astype(jnp.float32)
     half = col_width // LANES
 
     def pick_cols(j):
@@ -100,8 +118,9 @@
         picks = []
         for j in range(rows // LANES):
             at = pl.ds(pl.multiple_of(step * tile + part * rows + j * LANES, LANES), LANES)
-            first = jnp.where(ids == pairs_ref[0:1, at], 1.0, 0.0)
-            second = jnp.where(ids == pairs_ref[1:2, at], 1.0, 0.0)
+            both = pairs_ref[:, at].astype(jnp.float32)
+            first = jnp.where(idsf == both[0:1], 1.0, 0.0)
+            second = jnp.where(idsf == both[1:2], 1.0, 0.0)
             picks.append((first - second).T.astype(jnp.bfloat16))
         pick = jnp.concatenate(picks, axis=0)
         total = None
@@ -172,10 +191,11 @@
     blocks = coords.shape[3]
     row_width = pairs.shape[1]
     col_width = row_width * feats // frames
-    labels = jnp.broadcast_to(walker_map[0][:, None], (walker_map.shape[1], blocks))
-    block = jnp.concatenate(
-        [jnp.swapaxes(coords[0], 0, 1), labels.astype(coords.dtype)[None]], axis=0
-    )
+    own = jnp.swapaxes(coords[0], 0, 1)
+    count = own.shape[1]
+    labels = jnp.pad(walker_map.astype(own.dtype), ((0, count - 1), (0, blocks - count)))
+    block = jnp.concatenate([own, labels[None]], axis=0)
+    pairs = lax.optimization_barrier(pairs.astype(own.dtype))
     held, cols = gather_all(block, pairs)
     replicas = held.shape[2]
     samples = frames * replicas
@@ -183,7 +203,7 @@
     vmem = pl.BlockSpec(memory_space=pltpu.VMEM)
     hbm = pl.BlockSpec(memory_space=pl.ANY)
     return pl.pallas_call(
-        functools.partial(covariances, frames // 3, tile, chunk),
+        functools.partial(covariances, frames // 3, count, tile, chunk),
         out_shape=[jax.ShapeDtypeStruct((row_width, col_width), jnp.float32)] * 2,
         in_specs=[pl.BlockSpec(memory_space=pltpu.SMEM), vmem, vmem, vmem],
         out_specs=[hbm, hbm],

time: 52.3 us -> 49.8 us (0.952)
  waiting for transfers between devices: 10 us -> 8.63 us
  local copies, waits for them, and re-layouts: 0.88 us -> 0.07 us
    ppermute x5, starting transfers between devices: 9.96 us -> 6.7 us  [swap(): return lax.ppermute(x, axis, [(i, i ^ bit) for i in range(n)])]
    ppermute x5, waiting for transfers between devices: 10 us -> 6.96 us  [swap(): return lax.ppermute(x, axis, [(i, i ^ bit) for i in range(n)])]
    ppermute x0 -> x1, starting transfers between devices: none -> 2.9 us  [corner(): return lax.ppermute(x, ('frame', 'feat'), both)]
    ppermute x0 -> x1, waiting for transfers between devices: none -> 1.67 us  [corner(): return lax.ppermute(x, ('frame', 'feat'), both)]
    unnamed x2 -> x0, local copies, waits for them, and re-layouts: 0.75 us -> none
  transfers between devices with their start and end apart: 5 -> 6, of which waited for: 5 -> 6; matrix products, arithmetic and copies ran while one was open for 1% -> 2% of each run, Pallas kernels for 0% -> 0%
where the time goes in v3:
time: 49.8 us; the launch traced here: 49.5 us
  Pallas kernels  28 us (56%)
  starting transfers between devices  9.6 us (19%)
  waiting for transfers between devices  8.63 us (17%)
  other arithmetic  2.3 us (5%)
  between operations  0.92 us (2%)
    pallas_call x1, Pallas kernels, per_device(): pl.pallas_call(functools.partial(covariances, frames // 3, count, tile, c...  28 us
    ppermute x5, waiting for transfers between devices, swap(): return lax.ppermute(x, axis, [(i, i ^ bit) for i in range(n)])  6.96 us
    ppermute x5, starting transfers between devices, swap(): return lax.ppermute(x, axis, [(i, i ^ bit) for i in range(n)])  6.7 us
    ppermute x1, starting transfers between devices, corner(): return lax.ppermute(x, ('frame', 'feat'), both)  2.9 us
    ppermute x1, waiting for transfers between devices, corner(): return lax.ppermute(x, ('frame', 'feat'), both)  1.67 us
  transfers between devices with their start and end apart: 6, of which 6 were waited for; matrix products, arithmetic and copies ran while one was open for 2% of the time, Pallas kernels for 0%

profile of v3, /device:TPU:0, one launch (start us, length us, event | category | flops | bytes accessed | tf_op | source)
XLA Modules:
  0.0 49.5 jit_solution(18006851910499937218)
XLA Ops:
  0.6 0.7 %convert_element_type.8 = bf16[1,16]{1,0:T(2,128)(2,1)S(1)} convert(s32[1,16]{1,0:T(1,128)} %param.4) | non-fusion elementwise | flops 16 | bytes 96 | tf_op jit(solution)/shard_map/convert_element_type | solution.py:196
  1.3 0.7 %fusion.3 = (bf16[1,1,4,16,128]{4,3,2,1,0:T(8,128)(2,1)S(1)}, bf16[1,4,16,128]{3,2,1,0:T(8,128)(2,1)S(1)}) fusion(bf16[1,16,128]{2,1,0:T(8,128)(2,1)S(1)} %pad_bitcast_fusion, bf16[3,16,128]{2,1,0:T(8,128)(2,1)} %bitcast.38), kind=kLoop, calls=%fused_computation.12 | loop fusion | flops 8192 | bytes 49152 | tf_op jit(solution)/shard_map/stack;broadcast_in_dim | solution.py:34
  2.0 4.1 %collective-permute-start = (bf16[1,4,16,128]{3,2,1,0:T(8,128)(2,1)S(1)}, bf16[1,4,16,128]{3,2,1,0:T(8,128)(2,1)S(1)}, u32[]{:S(2)}, u32[]{:S(2)}) collective-permute-start(bf16[1,4,16,128]{3,2,1,0:T(8,128)(2,1)S(1)} %get-tuple-element.5), channel_id=1, source_target_pairs={{0,16},{4,20},{8,24},{12,28},{16,0},{20,4},{24,8},{28,12},{1,17},{... | collective-permute-start | bytes 49160 | tf_op jit(solution)/shard_map/ppermute | solution.py:20
  6.1 0.8 %convert_element_type.9.pairs_ref = bf16[2,4096]{1,0:T(2,128)(2,1)S(1)} convert(s32[2,4096]{1,0:T(2,128)} %param.5) | non-fusion elementwise | flops 8192 | bytes 49152 | tf_op jit(solution)/shard_map/convert_element_type | solution.py:198
  6.9 0.9 %collective-permute-done = bf16[1,4,16,128]{3,2,1,0:T(8,128)(2,1)S(1)} collective-permute-done((bf16[1,4,16,128]{3,2,1,0:T(8,128)(2,1)S(1)}, bf16[1,4,16,128]{3,2,1,0:T(8,128)(2,1)S(1)}, u32[]{:S(2)}, u32[]{:S(2)}) %collective-permute-start) | collective-permute-done | bytes 16416 | tf_op jit(solution)/shard_map/ppermute | solution.py:20
  7.8 1.9 %collective-permute-start.1 = (bf16[2,4,16,128]{3,2,1,0:T(8,128)(2,1)S(1)}, bf16[2,4,16,128]{3,2,1,0:T(8,128)(2,1)S(1)}, u32[]{:S(2)}, u32[]{:S(2)}) collective-permute-start(bf16[2,4,16,128]{3,2,1,0:T(8,128)(2,1)S(1)} %get-tuple-element.3), channel_id=1, source_target_pairs={{0,8},{4,12},{8,0},{12,4},{16,24},{20,28},{24,16},{28,20},{1,9},{5... | collective-permute-start | bytes 98312 | tf_op jit(solution)/shard_map/ppermute | solution.py:20
  9.8 2.0 %collective-permute-done.1 = bf16[2,4,16,128]{3,2,1,0:T(8,128)(2,1)S(1)} collective-permute-done((bf16[2,4,16,128]{3,2,1,0:T(8,128)(2,1)S(1)}, bf16[2,4,16,128]{3,2,1,0:T(8,128)(2,1)S(1)}, u32[]{:S(2)}, u32[]{:S(2)}) %collective-permute-start.1) | collective-permute-done | bytes 32800 | tf_op jit(solution)/shard_map/ppermute | solution.py:20
  11.7 2.9 %collective-permute-start.4 = (bf16[4,4,16,128]{3,2,1,0:T(8,128)(2,1)S(1)}, bf16[4,4,16,128]{3,2,1,0:T(8,128)(2,1)S(1)}, u32[]{:S(2)}, u32[]{:S(2)}) collective-permute-start(bf16[4,4,16,128]{3,2,1,0:T(8,128)(2,1)S(1)} %bitcast.31), channel_id=1, source_target_pairs={{0,6},{1,7},{2,4},{3,5},{4,2},{5,3},{6,0},{7,1},{8,14},{9,15},{10,... | collective-permute-start | bytes 196616 | tf_op jit(solution)/shard_map/ppermute | solution.py:51
  14.6 0.5 %collective-permute-start.3 = (bf16[4,4,16,128]{3,2,1,0:T(8,128)(2,1)S(1)}, bf16[4,4,16,128]{3,2,1,0:T(8,128)(2,1)S(1)}, u32[]{:S(2)}, u32[]{:S(2)}) collective-permute-start(bf16[4,4,16,128]{3,2,1,0:T(8,128)(2,1)S(1)} %bitcast.32), channel_id=1, source_target_pairs={{0,4},{4,0},{8,12},{12,8},{16,20},{20,16},{24,28},{28,24},{1,5},{5... | collective-permute-start | bytes 196616 | tf_op jit(solution)/shard_map/ppermute | solution.py:20
  15.2 0.1 collective-permute-start.2
  15.3 1.7 %collective-permute-done.4 = bf16[4,4,16,128]{3,2,1,0:T(8,128)(2,1)S(1)} collective-permute-done((bf16[4,4,16,128]{3,2,1,0:T(8,128)(2,1)S(1)}, bf16[4,4,16,128]{3,2,1,0:T(8,128)(2,1)S(1)}, u32[]{:S(2)}, u32[]{:S(2)}) %collective-permute-start.4) | collective-permute-done | bytes 65568 | tf_op jit(solution)/shard_map/ppermute | solution.py:51
  17.0 1.9 %collective-permute-done.3 = bf16[4,4,16,128]{3,2,1,0:T(8,128)(2,1)S(1)} collective-permute-done((bf16[4,4,16,128]{3,2,1,0:T(8,128)(2,1)S(1)}, bf16[4,4,16,128]{3,2,1,0:T(8,128)(2,1)S(1)}, u32[]{:S(2)}, u32[]{:S(2)}) %collective-permute-start.3) | collective-permute-done | bytes 65568 | tf_op jit(solution)/shard_map/ppermute | solution.py:20
  18.9 0.6 %collective-permute-done.2 = bf16[288,128]{1,0:T(8,128)(2,1)S(1)} collective-permute-done((bf16[288,128]{1,0:T(8,128)(2,1)S(1)}, bf16[288,128]{1,0:T(8,128)(2,1)S(1)}, u32[]{:S(2)}, u32[]{:S(2)}) %collective-permute-start.2) | collective-permute-done | bytes 73760 | tf_op jit(solution)/shard_map/ppermute | solution.py:20
  19.6 0.1 collective-permute-start.5
  19.7 1.5 %collective-permute-done.5 = bf16[1056,128]{1,0:T(8,128)(2,1)S(1)} collective-permute-done((bf16[1056,128]{1,0:T(8,128)(2,1)S(1)}, bf16[1056,128]{1,0:T(8,128)(2,1)S(1)}, u32[]{:S(2)}, u32[]{:S(2)}) %collective-permute-start.5) | collective-permute-done | bytes 270368 | tf_op jit(solution)/shard_map/ppermute | solution.py:20
  21.3 0.1 pad_maximum_fusion.y_ref
  21.4 28.0 %shard_map.50 = (f32[4096,2048]{1,0:T(8,128)}, f32[4096,2048]{1,0:T(8,128)}) custom-call(s32[1]{0:T(128)} %bitcast.f_ref, bf16[8,4,64,128]{3,2,1,0:T(8,128)(2,1)S(1)} %pad_maximum_fusion.y_ref, bf16[2,4096]{1,0:T(2,128)(2,1)S(1)} %convert_element_type.9.pairs_ref, bf16[32,128]{1,0:T(8,128)(2,1)S(1)} %slice_select_fusion.cols_ref), custom_call_target="tpu_custom_call" | custom-call | tf_op jit(solution)/shard_map/pallas_call | solution.py:205
  (15 shorter events, 0.2 us)
Async XLA Ops:
  2.0 5.8 %collective-permute-start = (bf16[1,4,16,128]{3,2,1,0:T(8,128)(2,1)S(1)}, bf16[1,4,16,128]{3,2,1,0:T(8,128)(2,1)S(1)}, u32[]{:S(2)}, u32[]{:S(2)}) collective-permute-start(bf16[1,4,16,128]{3,2,1,0:T(8,128)(2,1)S(1)} %get-tuple-element.5), channel_id=1, source_target_pairs={{0,16},{4,20},{8,24},{12,28},{16,0},{20,4},{24,8},{28,12},{1,17},{... | collective-permute-start | bytes 49160 | tf_op jit(solution)/shard_map/ppermute | solution.py:20
  7.8 3.9 %collective-permute-start.1 = (bf16[2,4,16,128]{3,2,1,0:T(8,128)(2,1)S(1)}, bf16[2,4,16,128]{3,2,1,0:T(8,128)(2,1)S(1)}, u32[]{:S(2)}, u32[]{:S(2)}) collective-permute-start(bf16[2,4,16,128]{3,2,1,0:T(8,128)(2,1)S(1)} %get-tuple-element.3), channel_id=1, source_target_pairs={{0,8},{4,12},{8,0},{12,4},{16,24},{20,28},{24,16},{28,20},{1,9},{5... | collective-permute-start | bytes 98312 | tf_op jit(solution)/shard_map/ppermute | solution.py:20
  11.7 5.2 %collective-permute-start.4 = (bf16[4,4,16,128]{3,2,1,0:T(8,128)(2,1)S(1)}, bf16[4,4,16,128]{3,2,1,0:T(8,128)(2,1)S(1)}, u32[]{:S(2)}, u32[]{:S(2)}) collective-permute-start(bf16[4,4,16,128]{3,2,1,0:T(8,128)(2,1)S(1)} %bitcast.31), channel_id=1, source_target_pairs={{0,6},{1,7},{2,4},{3,5},{4,2},{5,3},{6,0},{7,1},{8,14},{9,15},{10,... | collective-permute-start | bytes 196616 | tf_op jit(solution)/shard_map/ppermute | solution.py:51
  14.6 4.3 %collective-permute-start.3 = (bf16[4,4,16,128]{3,2,1,0:T(8,128)(2,1)S(1)}, bf16[4,4,16,128]{3,2,1,0:T(8,128)(2,1)S(1)}, u32[]{:S(2)}, u32[]{:S(2)}) collective-permute-start(bf16[4,4,16,128]{3,2,1,0:T(8,128)(2,1)S(1)} %bitcast.32), channel_id=1, source_target_pairs={{0,4},{4,0},{8,12},{12,8},{16,20},{20,16},{24,28},{28,24},{1,5},{5... | collective-permute-start | bytes 196616 | tf_op jit(solution)/shard_map/ppermute | solution.py:20
  15.2 4.4 %collective-permute-start.2 = (bf16[288,128]{1,0:T(8,128)(2,1)S(1)}, bf16[288,128]{1,0:T(8,128)(2,1)S(1)}, u32[]{:S(2)}, u32[]{:S(2)}) collective-permute-start(bf16[288,128]{1,0:T(8,128)(2,1)S(1)} %pad_maximum_fusion.3), channel_id=1, source_target_pairs={{0,2},{1,3},{2,0},{3,1},{4,6},{5,7},{6,4},{7,5},{8,10},{9,11},{10,... | collective-permute-start | bytes 221192 | tf_op jit(solution)/shard_map/ppermute | solution.py:20
  19.6 1.6 %collective-permute-start.5 = (bf16[1056,128]{1,0:T(8,128)(2,1)S(1)}, bf16[1056,128]{1,0:T(8,128)(2,1)S(1)}, u32[]{:S(2)}, u32[]{:S(2)}) collective-permute-start(bf16[1056,128]{1,0:T(8,128)(2,1)S(1)} %pad_maximum_fusion.1), channel_id=1, source_target_pairs={{0,1},{1,0},{2,3},{3,2},{4,5},{5,4},{6,7},{7,6},{8,9},{9,8},{10,11... | collective-permute-start | bytes 811016 | tf_op jit(solution)/shard_map/ppermute | solution.py:20

commit v4 on v3

--- a/solution.py
+++ b/solution.py
@@ -76,6 +76,7 @@
     late = lag * replicas
     f = f_ref[0]
     sides = (la_ref, lb_ref)
+    slots = out_ref.shape[0]
 
     walkers = lax.broadcasted_iota(jnp.int32, (replicas, blocks), 0).astype(jnp.float32)
     for t in range(frames):
@@ -113,11 +114,10 @@
             mean = jnp.sum(values, axis=0, keepdims=True) * (1.0 / samples)
             r_ref[:, k : k + wide] = (values - mean).astype(jnp.bfloat16)
 
-    def left(step, l_ref, part, parts):
-        rows = tile // parts
+    def left(step, l_ref):
         picks = []
-        for j in range(rows // LANES):
-            at = pl.ds(pl.multiple_of(step * tile + part * rows + j * LANES, LANES), LANES)
+        for j in range(tile // LANES):
+            at = pl.ds(step * tile + j * LANES, LANES)
             both = pairs_ref[:, at].astype(jnp.float32)
             first = jnp.where(idsf == both[0:1], 1.0, 0.0)
             second = jnp.where(idsf == both[1:2], 1.0, 0.0)
@@ -130,10 +130,10 @@
             total = d * d if total is None else total + d * d
         values = root(total)
         mean = jnp.sum(values, axis=1, keepdims=True) * (1.0 / samples)
-        l_ref[part * rows : (part + 1) * rows, :] = (values - mean).astype(jnp.bfloat16)
+        l_ref[...] = (values - mean).astype(jnp.bfloat16)
 
     def copies(step, slot, n):
-        rows = pl.ds(pl.multiple_of(step * tile, tile), tile)
+        rows = pl.ds(step * tile, tile)
         at = pl.ds(n * chunk, chunk)
         return [
             pltpu.make_async_copy(
@@ -151,39 +151,38 @@
             l_ref[:, :early], r_ref[late:, at], preferred_element_type=jnp.float32
         ) * (1.0 / early)
 
-    def round_of(step, slot, first=False, wait=True, last=False):
-        if wait:
-            for n in range(chunks):
-                for copy in copies(step - 2, slot, n):
-                    copy.wait()
+    def send(step, slot, n):
+        for copy in copies(step, slot, n):
+            copy.start()
+
+    def collect(step):
         for n in range(chunks):
-            products(sides[slot], slot, n)
-            if first and n + 1 < chunks:
-                right(n + 1)
-            if not last:
-                left(step + 1, sides[1 - slot], n, chunks)
-            for copy in copies(step, slot, n):
-                copy.start()
-
-    left(0, la_ref, 0, 1)
+            for copy in copies(step, step % slots, n):
+                copy.wait()
+
+    left(0, la_ref)
     right(0)
-    if steps % 2:
-        raise ValueError("odd steps")
-    round_of(0, 0, first=True, wait=False)
-    round_of(1, 1, wait=False, last=steps == 2)
-    if steps > 2:
-        def body(i, carry):
-            round_of(2 * i, 0)
-            round_of(2 * i + 1, 1)
-            return carry
-
-        lax.fori_loop(1, steps // 2 - 1, body, 0)
-        round_of(steps - 2, 0)
-        round_of(steps - 1, 1, last=True)
-    for step in (steps - 2, steps - 1):
+    left(1, lb_ref)
+    for n in range(chunks):
+        if n + 1 < chunks:
+            right(n + 1)
+        products(la_ref, 0, n)
+        send(0, 0, n)
+        if n + 1 == chunks and steps > 2:
+            left(2, la_ref)
+        products(lb_ref, 1, n)
+        send(1, 1, n)
+    for step in range(2, steps):
+        if step >= slots and step % 2 == 0:
+            for old in range(step - slots, min(step - slots + 2, steps)):
+                collect(old)
         for n in range(chunks):
-            for copy in copies(step, step % 2, n):
-                copy.wait()
+            products(sides[step % 2], step % slots, n)
+            if step + 1 < steps and n == 0:
+                left(step + 1, sides[(step + 1) % 2])
+            send(step, step % slots, n)
+    for step in range(steps - slots, steps):
+        collect(step)
 
 
 def per_device(coords, walker_map, pairs):
@@ -200,6 +199,7 @@
     replicas = held.shape[2]
     samples = frames * replicas
     tile, chunk = divisor(row_width // 2, 512), divisor(col_width, 512)
+    slots = min(row_width // tile, 4)
     vmem = pl.BlockSpec(memory_space=pltpu.VMEM)
     hbm = pl.BlockSpec(memory_space=pl.ANY)
     return pl.pallas_call(
@@ -213,8 +213,8 @@
             pltpu.VMEM((samples, col_width), jnp.bfloat16),
             pltpu.VMEM((tile, samples), jnp.bfloat16),
             pltpu.VMEM((tile, samples), jnp.bfloat16),
-            pltpu.VMEM((2, 2, tile, col_width), jnp.float32),
-            pltpu.SemaphoreType.DMA((2, 2, col_width // chunk)),
+            pltpu.VMEM((slots, 2, tile, col_width), jnp.float32),
+            pltpu.SemaphoreType.DMA((slots, 2, col_width // chunk)),
         ],
         compiler_params=pltpu.CompilerParams(vmem_limit_bytes=52 << 20),
     )(lax.axis_index("frame").astype(jnp.int32).reshape(1), held, pairs, cols)

time: 49.8 us -> 48.1 us (0.966)
  Pallas kernels: 28 us -> 26.3 us
    pallas_call x1, Pallas kernels: 28 us -> 26.3 us  [per_device(): pl.pallas_call(functools.partial(covariances, frames // 3, count, tile, c...]
where the time goes in v4:
time: 48.1 us; the launch traced here: 47.8 us
  Pallas kernels  26.3 us (55%)
  starting transfers between devices  9.6 us (20%)
  waiting for transfers between devices  8.63 us (18%)
  other arithmetic  2.3 us (5%)
  between operations  0.92 us (2%)
    pallas_call x1, Pallas kernels, per_device(): pl.pallas_call(functools.partial(covariances, frames // 3, count, tile, c...  26.3 us
    ppermute x5, waiting for transfers between devices, swap(): return lax.ppermute(x, axis, [(i, i ^ bit) for i in range(n)])  6.96 us
    ppermute x5, starting transfers between devices, swap(): return lax.ppermute(x, axis, [(i, i ^ bit) for i in range(n)])  6.7 us
    ppermute x1, starting transfers between devices, corner(): return lax.ppermute(x, ('frame', 'feat'), both)  2.9 us
    ppermute x1, waiting for transfers between devices, corner(): return lax.ppermute(x, ('frame', 'feat'), both)  1.67 us
  transfers between devices with their start and end apart: 6, of which 6 were waited for; matrix products, arithmetic and copies ran while one was open for 2% of the time, Pallas kernels for 0%

profile of v4, /device:TPU:0, one launch (start us, length us, event | category | flops | bytes accessed | tf_op | source)
XLA Modules:
  0.0 47.8 jit_solution(14072319958222908628)
XLA Ops:
  0.6 0.7 %convert_element_type.8 = bf16[1,16]{1,0:T(2,128)(2,1)S(1)} convert(s32[1,16]{1,0:T(1,128)} %param.4) | non-fusion elementwise | flops 16 | bytes 96 | tf_op jit(solution)/shard_map/convert_element_type | solution.py:195
  1.3 0.7 %fusion.3 = (bf16[1,1,4,16,128]{4,3,2,1,0:T(8,128)(2,1)S(1)}, bf16[1,4,16,128]{3,2,1,0:T(8,128)(2,1)S(1)}) fusion(bf16[1,16,128]{2,1,0:T(8,128)(2,1)S(1)} %pad_bitcast_fusion, bf16[3,16,128]{2,1,0:T(8,128)(2,1)} %bitcast.38), kind=kLoop, calls=%fused_computation.12 | loop fusion | flops 8192 | bytes 49152 | tf_op jit(solution)/shard_map/stack;broadcast_in_dim | solution.py:34
  2.0 4.1 %collective-permute-start = (bf16[1,4,16,128]{3,2,1,0:T(8,128)(2,1)S(1)}, bf16[1,4,16,128]{3,2,1,0:T(8,128)(2,1)S(1)}, u32[]{:S(2)}, u32[]{:S(2)}) collective-permute-start(bf16[1,4,16,128]{3,2,1,0:T(8,128)(2,1)S(1)} %get-tuple-element.5), channel_id=1, source_target_pairs={{0,16},{4,20},{8,24},{12,28},{16,0},{20,4},{24,8},{28,12},{1,17},{... | collective-permute-start | bytes 49160 | tf_op jit(solution)/shard_map/ppermute | solution.py:20
  6.1 0.8 %convert_element_type.9.pairs_ref = bf16[2,4096]{1,0:T(2,128)(2,1)S(1)} convert(s32[2,4096]{1,0:T(2,128)} %param.5) | non-fusion elementwise | flops 8192 | bytes 49152 | tf_op jit(solution)/shard_map/convert_element_type | solution.py:197
  6.9 0.9 %collective-permute-done = bf16[1,4,16,128]{3,2,1,0:T(8,128)(2,1)S(1)} collective-permute-done((bf16[1,4,16,128]{3,2,1,0:T(8,128)(2,1)S(1)}, bf16[1,4,16,128]{3,2,1,0:T(8,128)(2,1)S(1)}, u32[]{:S(2)}, u32[]{:S(2)}) %collective-permute-start) | collective-permute-done | bytes 16416 | tf_op jit(solution)/shard_map/ppermute | solution.py:20
  7.8 1.9 %collective-permute-start.1 = (bf16[2,4,16,128]{3,2,1,0:T(8,128)(2,1)S(1)}, bf16[2,4,16,128]{3,2,1,0:T(8,128)(2,1)S(1)}, u32[]{:S(2)}, u32[]{:S(2)}) collective-permute-start(bf16[2,4,16,128]{3,2,1,0:T(8,128)(2,1)S(1)} %get-tuple-element.3), channel_id=1, source_target_pairs={{0,8},{4,12},{8,0},{12,4},{16,24},{20,28},{24,16},{28,20},{1,9},{5... | collective-permute-start | bytes 98312 | tf_op jit(solution)/shard_map/ppermute | solution.py:20
  9.8 2.0 %collective-permute-done.1 = bf16[2,4,16,128]{3,2,1,0:T(8,128)(2,1)S(1)} collective-permute-done((bf16[2,4,16,128]{3,2,1,0:T(8,128)(2,1)S(1)}, bf16[2,4,16,128]{3,2,1,0:T(8,128)(2,1)S(1)}, u32[]{:S(2)}, u32[]{:S(2)}) %collective-permute-start.1) | collective-permute-done | bytes 32800 | tf_op jit(solution)/shard_map/ppermute | solution.py:20
  11.7 2.9 %collective-permute-start.4 = (bf16[4,4,16,128]{3,2,1,0:T(8,128)(2,1)S(1)}, bf16[4,4,16,128]{3,2,1,0:T(8,128)(2,1)S(1)}, u32[]{:S(2)}, u32[]{:S(2)}) collective-permute-start(bf16[4,4,16,128]{3,2,1,0:T(8,128)(2,1)S(1)} %bitcast.31), channel_id=1, source_target_pairs={{0,6},{1,7},{2,4},{3,5},{4,2},{5,3},{6,0},{7,1},{8,14},{9,15},{10,... | collective-permute-start | bytes 196616 | tf_op jit(solution)/shard_map/ppermute | solution.py:51
  14.6 0.5 %collective-permute-start.3 = (bf16[4,4,16,128]{3,2,1,0:T(8,128)(2,1)S(1)}, bf16[4,4,16,128]{3,2,1,0:T(8,128)(2,1)S(1)}, u32[]{:S(2)}, u32[]{:S(2)}) collective-permute-start(bf16[4,4,16,128]{3,2,1,0:T(8,128)(2,1)S(1)} %bitcast.32), channel_id=1, source_target_pairs={{0,4},{4,0},{8,12},{12,8},{16,20},{20,16},{24,28},{28,24},{1,5},{5... | collective-permute-start | bytes 196616 | tf_op jit(solution)/shard_map/ppermute | solution.py:20
  15.2 0.1 collective-permute-start.2
  15.3 1.7 %collective-permute-done.4 = bf16[4,4,16,128]{3,2,1,0:T(8,128)(2,1)S(1)} collective-permute-done((bf16[4,4,16,128]{3,2,1,0:T(8,128)(2,1)S(1)}, bf16[4,4,16,128]{3,2,1,0:T(8,128)(2,1)S(1)}, u32[]{:S(2)}, u32[]{:S(2)}) %collective-permute-start.4) | collective-permute-done | bytes 65568 | tf_op jit(solution)/shard_map/ppermute | solution.py:51
  17.0 1.9 %collective-permute-done.3 = bf16[4,4,16,128]{3,2,1,0:T(8,128)(2,1)S(1)} collective-permute-done((bf16[4,4,16,128]{3,2,1,0:T(8,128)(2,1)S(1)}, bf16[4,4,16,128]{3,2,1,0:T(8,128)(2,1)S(1)}, u32[]{:S(2)}, u32[]{:S(2)}) %collective-permute-start.3) | collective-permute-done | bytes 65568 | tf_op jit(solution)/shard_map/ppermute | solution.py:20
  18.9 0.6 %collective-permute-done.2 = bf16[288,128]{1,0:T(8,128)(2,1)S(1)} collective-permute-done((bf16[288,128]{1,0:T(8,128)(2,1)S(1)}, bf16[288,128]{1,0:T(8,128)(2,1)S(1)}, u32[]{:S(2)}, u32[]{:S(2)}) %collective-permute-start.2) | collective-permute-done | bytes 73760 | tf_op jit(solution)/shard_map/ppermute | solution.py:20
  19.6 0.1 collective-permute-start.5
  19.7 1.5 %collective-permute-done.5 = bf16[1056,128]{1,0:T(8,128)(2,1)S(1)} collective-permute-done((bf16[1056,128]{1,0:T(8,128)(2,1)S(1)}, bf16[1056,128]{1,0:T(8,128)(2,1)S(1)}, u32[]{:S(2)}, u32[]{:S(2)}) %collective-permute-start.5) | collective-permute-done | bytes 270368 | tf_op jit(solution)/shard_map/ppermute | solution.py:20
  21.3 0.1 pad_maximum_fusion.y_ref
  21.4 26.3 %shard_map.50 = (f32[4096,2048]{1,0:T(8,128)}, f32[4096,2048]{1,0:T(8,128)}) custom-call(s32[1]{0:T(128)} %bitcast.f_ref, bf16[8,4,64,128]{3,2,1,0:T(8,128)(2,1)S(1)} %pad_maximum_fusion.y_ref, bf16[2,4096]{1,0:T(2,128)(2,1)S(1)} %convert_element_type.9.pairs_ref, bf16[32,128]{1,0:T(8,128)(2,1)S(1)} %slice_select_fusion.cols_ref), custom_call_target="tpu_custom_call" | custom-call | tf_op jit(solution)/shard_map/pallas_call | solution.py:205
  (15 shorter events, 0.2 us)
Async XLA Ops:
  2.0 5.8 %collective-permute-start = (bf16[1,4,16,128]{3,2,1,0:T(8,128)(2,1)S(1)}, bf16[1,4,16,128]{3,2,1,0:T(8,128)(2,1)S(1)}, u32[]{:S(2)}, u32[]{:S(2)}) collective-permute-start(bf16[1,4,16,128]{3,2,1,0:T(8,128)(2,1)S(1)} %get-tuple-element.5), channel_id=1, source_target_pairs={{0,16},{4,20},{8,24},{12,28},{16,0},{20,4},{24,8},{28,12},{1,17},{... | collective-permute-start | bytes 49160 | tf_op jit(solution)/shard_map/ppermute | solution.py:20
  7.8 3.9 %collective-permute-start.1 = (bf16[2,4,16,128]{3,2,1,0:T(8,128)(2,1)S(1)}, bf16[2,4,16,128]{3,2,1,0:T(8,128)(2,1)S(1)}, u32[]{:S(2)}, u32[]{:S(2)}) collective-permute-start(bf16[2,4,16,128]{3,2,1,0:T(8,128)(2,1)S(1)} %get-tuple-element.3), channel_id=1, source_target_pairs={{0,8},{4,12},{8,0},{12,4},{16,24},{20,28},{24,16},{28,20},{1,9},{5... | collective-permute-start | bytes 98312 | tf_op jit(solution)/shard_map/ppermute | solution.py:20
  11.7 5.2 %collective-permute-start.4 = (bf16[4,4,16,128]{3,2,1,0:T(8,128)(2,1)S(1)}, bf16[4,4,16,128]{3,2,1,0:T(8,128)(2,1)S(1)}, u32[]{:S(2)}, u32[]{:S(2)}) collective-permute-start(bf16[4,4,16,128]{3,2,1,0:T(8,128)(2,1)S(1)} %bitcast.31), channel_id=1, source_target_pairs={{0,6},{1,7},{2,4},{3,5},{4,2},{5,3},{6,0},{7,1},{8,14},{9,15},{10,... | collective-permute-start | bytes 196616 | tf_op jit(solution)/shard_map/ppermute | solution.py:51
  14.6 4.3 %collective-permute-start.3 = (bf16[4,4,16,128]{3,2,1,0:T(8,128)(2,1)S(1)}, bf16[4,4,16,128]{3,2,1,0:T(8,128)(2,1)S(1)}, u32[]{:S(2)}, u32[]{:S(2)}) collective-permute-start(bf16[4,4,16,128]{3,2,1,0:T(8,128)(2,1)S(1)} %bitcast.32), channel_id=1, source_target_pairs={{0,4},{4,0},{8,12},{12,8},{16,20},{20,16},{24,28},{28,24},{1,5},{5... | collective-permute-start | bytes 196616 | tf_op jit(solution)/shard_map/ppermute | solution.py:20
  15.2 4.4 %collective-permute-start.2 = (bf16[288,128]{1,0:T(8,128)(2,1)S(1)}, bf16[288,128]{1,0:T(8,128)(2,1)S(1)}, u32[]{:S(2)}, u32[]{:S(2)}) collective-permute-start(bf16[288,128]{1,0:T(8,128)(2,1)S(1)} %pad_maximum_fusion.3), channel_id=1, source_target_pairs={{0,2},{1,3},{2,0},{3,1},{4,6},{5,7},{6,4},{7,5},{8,10},{9,11},{10,... | collective-permute-start | bytes 221192 | tf_op jit(solution)/shard_map/ppermute | solution.py:20
  19.6 1.6 %collective-permute-start.5 = (bf16[1056,128]{1,0:T(8,128)(2,1)S(1)}, bf16[1056,128]{1,0:T(8,128)(2,1)S(1)}, u32[]{:S(2)}, u32[]{:S(2)}) collective-permute-start(bf16[1056,128]{1,0:T(8,128)(2,1)S(1)} %pad_maximum_fusion.1), channel_id=1, source_target_pairs={{0,1},{1,0},{2,3},{3,2},{4,5},{5,4},{6,7},{7,6},{8,9},{9,8},{10,11... | collective-permute-start | bytes 811016 | tf_op jit(solution)/shard_map/ppermute | solution.py:20
